TPU v7x, 256 devices: a whole 4x4x8 slice. The times are simulated.
256 devices in a mesh: seq: 16 (over z, x_lo), head: 4 (over x_hi, core), req: 4 (over y).
Axes of the slice: x: 4 (x_hi: 2, x_lo: 2; x = x_hi * 2 + x_lo), y: 4, z: 8, core: 2. Of those that a mesh axis runs over, the one named last changes fastest.
Arguments:
- queries: bfloat16 [32768, 2560], P(('req', 'seq'), 'head'), parts along dimension 0, may hold values from -8 to 8
- keys: bfloat16 [32768, 2560], P(('req', 'seq'), 'head'), parts along dimension 0, may hold values from -8 to 8
- values: bfloat16 [32768, 2560], P(('req', 'seq'), 'head'), parts along dimension 0, may hold values from -8 to 8
- clip_ids: int32 [32768], P('req'), parts along dimension 0, may hold values from 0 to 3, never falling along the last dimension, each value on 1 to 3072 neighbouring positions
- plan: int32 [256], P('req'), parts along dimension 0, may hold values from 0 to 15, as said below
Outputs:
- attended: bfloat16 [32768, 2560], P(('req', 'seq'), 'head'), parts along dimension 0
- log_normalizer: float32 [20, 32768], P('head', ('req', 'seq')), parts along dimension 1
There are 4 independent parts, one for each index of `req`. A program takes and returns all parts, laid end to end along the dimension named above; each array names one. Nothing has to cross between parts.
Inputs may be any that keep to these rules, and one draw needn't show every extreme that they name: `plan`: every index along seq computes exactly 4 blocks, and of the 4 blocks held by one index of seq (blocks k * 4 to k * 4 + 3 on index k) at most 1 go to the same index; some pair of indices reaches 1. `clip_ids`: clip ids never fall along the tokens; each clip holds 1 to 3072 tokens and one holds exactly 3072.
All inputs are finite; a program needn't handle non-finite values.
Results may differ from a plain program's by a relative error of at most 0.007.
Values may be sent and summed in bfloat16 or wider, within the bound.
A program may use at most 128 MiB of HBM per device.

v0:
```python
import jax
import jax.numpy as jnp
from jax import lax
from jax.sharding import PartitionSpec as P

HD = 128
BLOCK = 128


def shards(queries, keys, values, clip_ids, plan):
    group_size = lax.axis_size("seq")
    rank_here = lax.axis_index("seq")
    tok_dev, width_dev = queries.shape
    blocks_dev = tok_dev // BLOCK
    blocks_all = plan.shape[0]
    capacity = (blocks_dev + group_size - 1) // group_size
    slot_count = group_size * capacity
    heads_dev = width_dev // HD
    score_scale = 1.0 / HD**0.5
    block_index = jnp.arange(blocks_all, dtype=jnp.int32)
    source = block_index // blocks_dev
    earlier = (
        (plan[None, :] == plan[:, None])
        & (source[None, :] == source[:, None])
        & (block_index[None, :] < block_index[:, None])
    )
    pair_rank = jnp.sum(earlier, axis=1)
    send_slot = plan * capacity + pair_rank
    recv_slot_all = source * capacity + pair_rank
    local_send = lax.dynamic_slice_in_dim(send_slot, rank_here * blocks_dev, blocks_dev)
    slot_range = jnp.arange(slot_count, dtype=jnp.int32)
    local_range = jnp.arange(blocks_dev, dtype=jnp.int32)
    send_match = slot_range[:, None] == local_send[None, :]
    send_pick = jnp.sum(send_match * local_range[None, :], axis=1)
    send_filled = jnp.any(send_match, axis=1)
    owned_here = plan == rank_here
    position = jnp.cumsum(owned_here.astype(jnp.int32)) - 1
    choose = (local_range[:, None] == position[None, :]) & owned_here[None, :]
    recv_pick = jnp.sum(choose * recv_slot_all[None, :], axis=1)
    back_match = slot_range[:, None] == recv_pick[None, :]
    back_pick = jnp.sum(back_match * local_range[None, :], axis=1)
    back_filled = jnp.any(back_match, axis=1)
    sort_key = plan * blocks_all + block_index
    packed_place = jnp.sum(sort_key[None, :] < sort_key[:, None], axis=1)
    packed_block = jnp.sum(
        (packed_place[None, :] == block_index[:, None]) * block_index[None, :], axis=1
    )
    packed_ids = jnp.take(clip_ids.reshape(blocks_all, BLOCK), packed_block, axis=0).reshape(-1)

    def pack_slots(tokens_dev, picked, filled):
        columns = tokens_dev.shape[1]
        blocked = jnp.take(tokens_dev.reshape(blocks_dev, BLOCK, columns), picked, axis=0)
        blocked = jnp.where(filled[:, None, None], blocked, jnp.zeros_like(blocked))
        return blocked.reshape(group_size, capacity, BLOCK, columns)

    def read_slots(arrived, picked):
        columns = arrived.shape[-1]
        blocked = jnp.take(arrived.reshape(slot_count, BLOCK, columns), picked, axis=0)
        return blocked.reshape(blocks_dev * BLOCK, columns)

    arrived = (
        lax.all_to_all(
            pack_slots(queries, send_pick, send_filled),
            "seq",
            split_axis=0,
            concat_axis=0,
            tiled=True,
        ),
        lax.all_to_all(
            pack_slots(keys, send_pick, send_filled), "seq", split_axis=0, concat_axis=0, tiled=True
        ),
        lax.all_to_all(
            pack_slots(values, send_pick, send_filled),
            "seq",
            split_axis=0,
            concat_axis=0,
            tiled=True,
        ),
    )
    query_rows = read_slots(arrived[0], recv_pick)
    loop_source = (read_slots(arrived[1], recv_pick), read_slots(arrived[2], recv_pick))
    query_ids = lax.dynamic_slice_in_dim(packed_ids, rank_here * tok_dev, tok_dev)
    query_heads = query_rows.reshape(tok_dev, heads_dev, HD)

    def attend_block(state, key_part, value_part, part_ids):
        running_max, running_sum, accumulated = state
        rows = key_part.shape[0]
        scores = (
            jnp.einsum(
                "qhd,khd->hqk",
                query_heads,
                key_part.reshape(rows, heads_dev, HD),
                preferred_element_type=jnp.float32,
            )
            * score_scale
        )
        same_clip = (query_ids[:, None] == part_ids[None, :])[None, :, :]
        masked = jnp.where(same_clip, scores, jnp.float32(-1e30))
        new_max = jnp.maximum(running_max, jnp.max(masked, axis=2))
        weights = jnp.where(same_clip, jnp.exp(masked - new_max[:, :, None]), jnp.float32(0.0))
        rescale = jnp.exp(running_max - new_max)
        running_sum = running_sum * rescale + jnp.sum(weights, axis=2)
        product = jnp.einsum(
            "hqk,khd->qhd",
            weights.astype(jnp.bfloat16),
            value_part.reshape(rows, heads_dev, HD),
            preferred_element_type=jnp.float32,
        )
        accumulated = accumulated * jnp.transpose(rescale)[:, :, None] + product
        return (new_max, running_sum, accumulated)

    start_state = (
        jnp.full((heads_dev, tok_dev), -1e30, jnp.float32),
        jnp.zeros((heads_dev, tok_dev), jnp.float32),
        jnp.zeros((tok_dev, heads_dev, HD), jnp.float32),
    )
    key_part = lax.all_gather(loop_source[0], "seq", axis=0, tiled=True)
    value_part = lax.all_gather(loop_source[1], "seq", axis=0, tiled=True)
    part_ids = packed_ids
    rows = key_part.shape[0]
    sub_count = rows // 512

    def scan_step(inner_state, inputs):
        return (attend_block(inner_state, inputs[0], inputs[1], inputs[2]), None)

    inputs = (
        key_part.reshape(sub_count, 512, width_dev),
        value_part.reshape(sub_count, 512, width_dev),
        part_ids.reshape(sub_count, 512),
    )
    final_state, unused = lax.scan(scan_step, start_state, inputs)
    running_max, running_sum, accumulated = final_state
    finished = (
        (accumulated / jnp.transpose(running_sum)[:, :, None])
        .astype(jnp.bfloat16)
        .reshape(tok_dev, width_dev)
    )
    log_totals = running_max + jnp.log(running_sum)
    returned = lax.all_to_all(
        pack_slots(finished, back_pick, back_filled), "seq", split_axis=0, concat_axis=0, tiled=True
    )
    attended = read_slots(returned, local_send)
    return (attended, log_totals)


def solution(mesh):
    return jax.shard_map(
        shards,
        mesh=mesh,
        in_specs=(
            P(("req", "seq"), "head"),
            P(("req", "seq"), "head"),
            P(("req", "seq"), "head"),
            P("req"),
            P("req"),
        ),
        out_specs=(P(("req", "seq"), "head"), P("head", ("req", "seq"))),
        check_vma=False,
    )
```

profile of v0, /device:TPU:1, one launch (start us, length us, event | category | flops | bytes accessed | tf_op | source)
XLA Modules:
  0.0 998.0 jit_solution(18444506933324885968)
XLA Ops:
  10.0 2.4 gather_fusion.3
  12.4 2.4 gather_fusion.5
  14.8 2.4 gather_fusion.1
  17.1 4.2 fusion.18
  21.4 70.5 %all_to_all.20 = bf16[16,1,128,640]{3,2,1,0:T(8,128)(2,1)} all-to-all(bf16[16,1,128,640]{3,2,1,0:T(8,128)(2,1)S(1)} %get-tuple-element.152), channel_id=1, replica_groups=mesh['seq'=16,'head'=4,'req'=4] {'seq'}, dimensions={0} | all-to-all | bytes 5242880 | tf_op jit(solution)/shard_map/all_to_all | solution.py:69
  91.9 65.4 %all_to_all.21 = bf16[16,1,128,640]{3,2,1,0:T(8,128)(2,1)} all-to-all(bf16[16,1,128,640]{3,2,1,0:T(8,128)(2,1)S(1)} %get-tuple-element.151), channel_id=1, replica_groups=mesh['seq'=16,'head'=4,'req'=4] {'seq'}, dimensions={0} | all-to-all | bytes 5242880 | tf_op jit(solution)/shard_map/all_to_all | solution.py:62
  157.3 4.6 all-to-all-start.2
  162.4 3.3 gather_fusion.2
  165.7 3.2 gather_fusion.4
  168.9 52.9 %all-to-all-done.2 = bf16[16,1,128,640]{3,2,1,0:T(8,128)(2,1)S(1)} async-done(((bf16[16,1,128,640]{3,2,1,0:T(8,128)(2,1)}), bf16[16,1,128,640]{3,2,1,0:T(8,128)(2,1)S(1)}, u32[]{:S(2)}, u32[]{:S(2)}) %all-to-all-start.2) | async-done | bytes 2621472 | tf_op jit(solution)/shard_map/all_to_all | solution.py:72
  221.8 1.5 gather_fusion.6
  223.3 2.8 broadcast_select_fusion.1
  232.2 218.2 %all-gather.3.cloned.1.call-done = bf16[8192,640]{1,0:T(8,128)(2,1)} async-done(((bf16[512,640]{1,0:T(8,128)(2,1)}), bf16[8192,640]{1,0:T(8,128)(2,1)}) %all-gather.3.cloned.1.call-update) | async-done | bytes 10485776 | tf_op jit(solution)/shard_map/all_gather | solution.py:117
  450.4 227.8 %all-gather.5.cloned.1.call-done = bf16[8192,640]{1,0:T(8,128)(2,1)} async-done(((bf16[512,640]{1,0:T(8,128)(2,1)}), bf16[8192,640]{1,0:T(8,128)(2,1)}) %all-gather.5.cloned.1.call-update) | async-done | bytes 10485776 | tf_op jit(solution)/shard_map/all_gather | solution.py:118
  678.2 236.1 %while.15 = (s32[]{:T(128)}, f32[5,512]{1,0:T(8,128)S(1)}, f32[5,512]{1,0:T(8,128)}, f32[512,5,128]{0,2,1:T(8,128)}, s32[512]{0:T(512)}, /*index=5*/s32[16,512]{...) while((s32[]{:T(128)}, f32[5,512]{1,0:T(8,128)S(1)}, ...), condition=%wide.region_11.14_spmd.clone, body=%wide.region_8.0_spmd.clone.sunk | while | flops 689388544 | bytes 42590440 | solution.py:131
  679.8 1.4 constant_dynamic-slice_fusion.6
  681.5 3.5 fusion.43
  685.3 5.4 fusion.47
  694.2 1.4 constant_dynamic-slice_fusion.6
  695.9 3.5 fusion.43
  699.7 5.8 fusion.47
  709.0 1.4 constant_dynamic-slice_fusion.6
  710.7 3.5 fusion.43
  714.5 5.8 fusion.47
  723.8 1.4 constant_dynamic-slice_fusion.6
  725.5 3.5 fusion.43
  729.2 5.8 fusion.47
  738.6 1.4 constant_dynamic-slice_fusion.6
  740.2 3.5 fusion.43
  744.0 5.8 fusion.47
  753.4 1.4 constant_dynamic-slice_fusion.6
  755.0 3.5 fusion.43
  758.8 5.8 fusion.47
  768.1 1.4 constant_dynamic-slice_fusion.6
  769.8 3.5 fusion.43
  773.6 5.8 fusion.47
  782.9 1.4 constant_dynamic-slice_fusion.6
  784.6 3.5 fusion.43
  788.4 5.8 fusion.47
  797.7 1.4 constant_dynamic-slice_fusion.6
  799.4 3.5 fusion.43
  803.1 5.8 fusion.47
  814.1 3.5 fusion.43
  817.9 5.8 fusion.47
  827.2 1.4 constant_dynamic-slice_fusion.6
  828.9 3.5 fusion.43
  832.7 5.8 fusion.47
  843.7 3.5 fusion.43
  847.5 5.8 fusion.47
  858.5 3.5 fusion.43
  862.3 5.8 fusion.47
  871.6 1.4 constant_dynamic-slice_fusion.6
  873.3 3.5 fusion.43
  877.0 5.8 fusion.47
  888.0 3.5 fusion.43
  891.8 5.8 fusion.47
  902.8 3.5 fusion.43
  906.6 5.8 fusion.47
  914.3 1.5 divide_convert_fusion
  918.0 1.9 fusion.17
  920.0 7.4 all-to-all-start.3
  928.0 59.6 %all-to-all-done.3 = bf16[16,1,128,640]{3,2,1,0:T(8,128)(2,1)S(1)} async-done(((bf16[16,1,128,640]{3,2,1,0:T(8,128)(2,1)}), bf16[16,1,128,640]{3,2,1,0:T(8,128)(2,1)S(1)}, u32[]{:S(2)}, u32[]{:S(2)}) %all-to-all-start.3) | async-done | bytes 2621472 | tf_op jit(solution)/shard_map/all_to_all | solution.py:139
  987.6 1.5 gather_fusion.8
  989.1 2.1 broadcast_select_fusion
  (353 shorter events, 83.4 us)
Async XLA Ops:
  7.2 2.8 copy-start
  10.0 2.4 copy-start.2
  12.4 2.4 copy-start.3
  14.8 2.4 copy-start.4
  157.3 4.7 copy-start.9
  157.3 64.6 %all-to-all-start.2 = ((bf16[16,1,128,640]{3,2,1,0:T(8,128)(2,1)}), bf16[16,1,128,640]{3,2,1,0:T(8,128)(2,1)S(1)}, u32[]{:S(2)}, u32[]{:S(2)}) async-start(bf16[16,1,128,640]{3,2,1,0:T(8,128)(2,1)} %get-tuple-element.150), calls=%async_computation.2 | async-start | bytes 5242880 | tf_op jit(solution)/shard_map/all_to_all | solution.py:72
  161.9 288.5 %all-gather.3.cloned.1.call-start = ((), (), s32[]{:S(2)}) async-start(), calls=%async_computation.4 | async-start | bytes 11141120 | tf_op jit(solution)/shard_map/all_gather | solution.py:117
  223.3 4.1 copy-start.5
  226.2 452.1 %all-gather.5.cloned.1.call-start = ((), (), s32[]{:S(2)}) async-start(), calls=%async_computation.5 | async-start | bytes 11141120 | tf_op jit(solution)/shard_map/all_gather | solution.py:118
  685.0 5.7 slice-start
  685.3 5.4 slice-start.1
  690.7 1.3 copy-start.6
  699.4 6.1 slice-start
  699.7 5.8 slice-start.1
  705.5 1.3 copy-start.6
  714.2 6.1 slice-start
  714.5 5.8 slice-start.1
  720.2 1.3 copy-start.6
  729.0 6.1 slice-start
  729.2 5.8 slice-start.1
  735.0 1.3 copy-start.6
  743.7 6.1 slice-start
  744.0 5.8 slice-start.1
  749.8 1.3 copy-start.6
  758.5 6.1 slice-start
  758.8 5.8 slice-start.1
  764.6 1.3 copy-start.6
  773.3 6.1 slice-start
  773.6 5.8 slice-start.1
  779.4 1.3 copy-start.6
  788.1 6.1 slice-start
  788.3 5.8 slice-start.1
  794.1 1.3 copy-start.6
  802.9 6.1 slice-start
  803.1 5.8 slice-start.1
  808.9 1.3 copy-start.6
  817.6 6.1 slice-start
  817.9 5.8 slice-start.1
  823.7 1.3 copy-start.6
  832.4 6.1 slice-start
  832.7 5.8 slice-start.1
  838.5 1.3 copy-start.6
  847.2 6.1 slice-start
  847.5 5.8 slice-start.1
  853.3 1.3 copy-start.6
  862.0 6.1 slice-start
  862.2 5.8 slice-start.1
  868.0 1.3 copy-start.6
  876.8 6.1 slice-start
  877.0 5.8 slice-start.1
  882.8 1.3 copy-start.6
  891.5 6.1 slice-start
  891.8 5.8 slice-start.1
  897.6 1.3 copy-start.6
  906.3 6.1 slice-start
  906.6 5.8 slice-start.1
  912.4 1.3 copy-start.6
  916.8 1.2 copy-start.11
  916.8 1.2 copy-start.12
  920.0 7.4 copy-start.14
  920.0 7.4 copy-start.8
  920.0 69.1 %copy-start.10 = (pred[4]{0:T(512)(128)(4,1)S(1)}, pred[4]{0:T(512)(128)(4,1)}, u32[]{:S(2)}) copy-start(pred[4]{0:T(512)(128)(4,1)} %get-tuple-element.142) | copy-start | bytes 16
  920.0 67.6 %all-to-all-start.3 = ((bf16[16,1,128,640]{3,2,1,0:T(8,128)(2,1)}), bf16[16,1,128,640]{3,2,1,0:T(8,128)(2,1)S(1)}, u32[]{:S(2)}, u32[]{:S(2)}) async-start(bf16[16,1,128,640]{3,2,1,0:T(8,128)(2,1)} %fusion.17), calls=%async_computation.3 | async-start | bytes 5242880 | tf_op jit(solution)/shard_map/all_to_all | solution.py:139
  927.4 63.8 %copy-start.1 = (bf16[512,640]{1,0:T(8,128)(2,1)S(1)}, bf16[512,640]{1,0:T(8,128)(2,1)}, u32[]{:S(2)}) copy-start(bf16[512,640]{1,0:T(8,128)(2,1)} %param.11) | copy-start | bytes 1966084
  (17 other events, 10.3 us)
Sparse Core Ops, SparseCore 0:
  226.3 224.0 all-gather.2
  452.7 225.4 all-gather.4
where the time goes:
time: 1000 us; the launch traced here: 998 us
  waiting for transfers between devices  559 us (56%)
  matrix products  148 us (15%)
  blocking collectives  136 us (14%)
  local copies, waits for them, and re-layouts  73.1 us (7%)
  other arithmetic  54 us (5%)
  between operations  14.3 us (1%)
  starting transfers between devices  12.1 us (1%)
    all_gather x1, waiting for transfers between devices, shards(): value_part = lax.all_gather(loop_source[1], 'seq', axis=0, tiled=True)  228 us
    all_gather x1, waiting for transfers between devices, shards(): key_part = lax.all_gather(loop_source[0], 'seq', axis=0, tiled=True)  218 us
    dot_general x16, matrix products, attend_block(): jnp.einsum('hqk,khd->qhd', weights.astype(jnp.bfloat16), value_part.resha...  92 us
    all_to_all x1, blocking collectives, shards(): lax.all_to_all(pack_slots(keys, send_pick, send_filled), 'seq', split_axi...  70.5 us
    all_to_all x1, blocking collectives, shards(): lax.all_to_all(pack_slots(queries, send_pick, send_filled), 'seq', split_...  65.4 us
    all_to_all x1, waiting for transfers between devices, shards(): lax.all_to_all(pack_slots(finished, back_pick, back_filled), 'seq', split...  59.6 us
    dot_general x16, matrix products, attend_block(): jnp.einsum('qhd,khd->hqk', query_heads, key_part.reshape(rows, heads_dev,...  55.7 us
    all_to_all x1, waiting for transfers between devices, shards(): lax.all_to_all(pack_slots(values, send_pick, send_filled), 'seq', split_a...  52.9 us
  transfers between devices with their start and end apart: 4, of which 4 were waited for; matrix products, arithmetic and copies ran while one was open for 1% of the time, Pallas kernels for 0%

commit v1 on v0

v1 whole, which is shorter than its diff:
```python
import functools

import jax
import jax.numpy as jnp
from jax import lax
from jax.experimental import pallas as pl
from jax.experimental.pallas import tpu as pltpu
from jax.sharding import PartitionSpec as P

HD = 128
ROWS = 512
HALF = 256
NZ = 8
REACH = 6
APART = 32768.0
SCALE = 1.0 / HD**0.5
TO_EXP2 = 1.4426950408889634 * SCALE
MESH = pl.DeviceIdType.MESH


def kernel(
    q_in, k_in, v_in, ids_ref, plan_ref,
    att, lg_out,
    kv, qu, ou, kv5, q5, o5, mk, m_ref, acc_ref, lg, lg5, lg_all, lg5_all,
    q_send, k_send, v_send, x_send, c_send, f_send, ch_send, c5_send, o_send, o5_send, lg_send, lg5_send,
    q_recv, kv_recv, x_recv, c_recv, f_recv, chl_recv, chr_recv, c5_recv, o_recv, o5_recv, lg_recv, lg5_recv,
):
    seq = lax.axis_index("seq")
    head = lax.axis_index("head")
    z, x = seq // 2, seq % 2
    xh, c = head // 2, head % 2
    g, i_head = z % 2, z // 2
    kb5 = 2 * z + c

    def at(zz, xx, cc):
        return {"seq": 2 * zz + xx, "head": 2 * xh + cc}

    def remote(src, dst, send, recv, where):
        return pltpu.make_async_remote_copy(
            src_ref=src, dst_ref=dst, send_sem=send, recv_sem=recv, device_id=where, device_id_type=MESH
        )

    def arrived(dst, recv):
        remote(dst, dst, recv, recv, at(z, x, 1 - c)).wait_recv()

    barrier = pltpu.get_barrier_semaphore()

    def greet(t, carry):
        other_seq, other_c = t // 2, t % 2

        @pl.when(jnp.logical_or(other_seq != seq, other_c != c))
        def _():
            pl.semaphore_signal(
                barrier, inc=1, device_id={"seq": other_seq, "head": 2 * xh + other_c}, device_id_type=MESH
            )

        return carry

    lax.fori_loop(0, 32, greet, 0)
    pl.semaphore_wait(barrier, 31)

    def piece(kind, j):
        cols = pl.ds(j * HD, HD)
        zt = 2 * j + c
        if kind == "k":
            return k_in.at[:, cols], kv.at[0, 2 * z + x], k_send.at[j], kv_recv.at[z], zt, 0
        if kind == "v":
            return v_in.at[:, cols], kv.at[1, 2 * z + x], v_send.at[j], kv_recv.at[z], zt, 1
        a = int(kind[1])
        return q_in.at[pl.ds(a * HALF, HALF), cols], qu.at[z], q_send.at[j, a], q_recv.at[z], zt, a

    def each_piece(do):
        for kind in ("k", "v", "q0", "q1"):
            for j in range(4):
                do(*piece(kind, j))

    def start_piece(src, dst, send, recv, zt, core):
        here = jnp.logical_and(zt == z, c == core)

        @pl.when(here)
        def _():
            pltpu.make_async_copy(src, dst, recv).start()

        @pl.when(jnp.logical_not(here))
        def _():
            remote(src, dst, send, recv, at(zt, x, core)).start()

    def sent_piece(src, dst, send, recv, zt, core):
        @pl.when(jnp.logical_not(jnp.logical_and(zt == z, c == core)))
        def _():
            remote(src, dst, send, recv, at(zt, x, core)).wait_send()

    cols5 = pl.ds(4 * HD, HD)

    def swap_copies():
        k_dst = 2 * z + x
        return (
            (k_in.at[:, cols5], kv5.at[k_dst, 0], 0),
            (v_in.at[:, cols5], kv5.at[k_dst, 1], 1),
            (q_in.at[:, cols5], q5, 2),
        )

    same = c == x

    def start_swap():
        for src, dst, n in swap_copies():

            @pl.when(same)
            def _():
                pltpu.make_async_copy(src, dst, f_recv.at[n]).start()

            @pl.when(jnp.logical_not(same))
            def _():
                remote(src, dst, f_send.at[n], f_recv.at[n], at(z, 1 - x, 1 - c)).start()

    def sent_swap():
        @pl.when(jnp.logical_not(same))
        def _():
            for src, dst, n in swap_copies():
                remote(src, dst, f_send.at[n], f_recv.at[n], at(z, 1 - x, 1 - c)).wait_send()

    start_swap()
    each_piece(start_piece)
    lg5[...] = jnp.zeros((8, HD), jnp.float32)

    ids = ids_ref[...]
    starts = [jnp.sum(jnp.sum(jnp.where(ids < n, 1.0, 0.0), axis=0, keepdims=True), axis=1, keepdims=True) for n in (1, 2, 3)]

    def clip_of(first, rows):
        pos = (first + lax.broadcasted_iota(jnp.int32, (rows, HD), 0)).astype(jnp.float32)
        clip = jnp.zeros((rows, HD), jnp.float32)
        for s in starts:
            clip = clip + jnp.where(pos >= s, 1.0, 0.0)
        return clip, lax.broadcasted_iota(jnp.int32, (rows, HD), 1).astype(jnp.float32)

    def fill(b, carry):
        clip, lane = clip_of(b * ROWS, ROWS)
        mk[b] = jnp.where(lane == clip, 0.0, jnp.where(lane < 4.0, 1.0, 0.0)).astype(jnp.bfloat16)
        return carry

    def block_in(src):
        return kv.at[c, 2 * src + x]

    def to_x(src):
        return remote(block_in(src), block_in(src), x_send.at[src], x_recv.at[src], at(z, 1 - x, c))

    def to_core(b):
        return remote(kv.at[c, b], kv.at[c, b], c_send.at[b], c_recv.at[b], at(z, x, 1 - c))

    def relay(d):
        src = (z + d + NZ) % NZ
        arrived(block_in(src), kv_recv.at[src])
        to_x(src).start()
        to_core(2 * src + x).start()

    def relay_x(d):
        src = (z + d + NZ) % NZ
        b = 2 * src + 1 - x
        arrived(kv.at[c, b], x_recv.at[src])
        to_core(b).start()

    def c5_copy(zz):
        b = 2 * zz + c
        return remote(kv5.at[b], kv5.at[b], c5_send.at[zz], c5_recv.at[b], at(z, x, 1 - c))

    def right(s):
        b = 2 * (z - s + 1) + c
        return remote(kv5.at[b], kv5.at[b], ch_send.at[0, s - 1], chl_recv.at[s - 1], at((z + 1) % NZ, x, c))

    def left(s):
        b = 2 * (z + s - 1) + c
        return remote(kv5.at[b], kv5.at[b], ch_send.at[1, s - 1], chr_recv.at[s - 1], at((z + NZ - 1) % NZ, x, c))

    def goes_right(s):
        return jnp.logical_and(z + 1 < NZ, z - s + 1 >= 0)

    def goes_left(s):
        return jnp.logical_and(z - 1 >= 0, z + s - 1 < NZ)

    lax.fori_loop(0, 16, fill, 0)
    order = (0, 1, -1, 2, -2, 3, -3, 4)
    for d in order[:3]:
        relay(d)
    arrived(kv5.at[kb5, 0], f_recv.at[0])
    arrived(kv5.at[kb5, 1], f_recv.at[1])
    c5_copy(z).start()

    @pl.when(goes_right(1))
    def _():
        right(1).start()

    @pl.when(goes_left(1))
    def _():
        left(1).start()

    for d in order[3:]:
        relay(d)
    for d in order:
        relay_x(d)
    for src in range(NZ):
        arrived(qu.at[src], q_recv.at[src])
    for b in range(16):
        arrived(kv.at[1 - c, b], c_recv.at[b])

    def chain(s):
        @pl.when(z - s >= 0)
        def _():
            b = 2 * (z - s) + c
            arrived(kv5.at[b], chl_recv.at[s - 1])
            c5_copy(z - s).start()

        if s < 3:

            @pl.when(goes_right(s + 1))
            def _():
                right(s + 1).start()

        @pl.when(z + s < NZ)
        def _():
            b = 2 * (z + s) + c
            arrived(kv5.at[b], chr_recv.at[s - 1])
            c5_copy(z + s).start()

        if s < 3:

            @pl.when(goes_left(s + 1))
            def _():
                left(s + 1).start()

    ones = jnp.ones((ROWS, HD), jnp.bfloat16)

    def attend(q, first, block, k_of, v_of):
        clip, lane = clip_of(first, HALF)
        mq = jnp.where(lane == clip, -APART, 0.0).astype(jnp.bfloat16)
        qa = jnp.concatenate([q, mq], axis=1)
        m_ref[...] = jnp.full((HALF, HD), -1e30, jnp.float32)
        acc_ref[...] = jnp.zeros((HALF, 2 * HD), jnp.float32)

        def step(b, carry):
            ka = jnp.concatenate([k_of(b), mk[b]], axis=1)
            s = lax.dot_general(qa, ka, (((1,), (1,)), ((), ())), preferred_element_type=jnp.float32)
            m_old = m_ref[...]
            m_new = jnp.maximum(m_old, jnp.max(s, axis=1, keepdims=True))
            alpha = jnp.exp2((m_old - m_new) * TO_EXP2)
            p = jnp.exp2((s - jnp.concatenate([m_new] * (ROWS // HD), axis=1)) * TO_EXP2)
            va = jnp.concatenate([v_of(b), ones], axis=1)
            pv = jnp.dot(p.astype(jnp.bfloat16), va, preferred_element_type=jnp.float32)
            acc_ref[...] = acc_ref[...] * jnp.concatenate([alpha, alpha], axis=1) + pv
            m_ref[...] = m_new
            return carry

        lax.fori_loop(jnp.maximum(block - REACH, 0), jnp.minimum(block + REACH + 1, 2 * NZ), step, 0)
        total = acc_ref[:, HD:]
        out = (acc_ref[:, :HD] / total).astype(jnp.bfloat16)
        log_total = m_ref[...] * SCALE + jnp.log(total)
        return out, jnp.transpose(log_total)[0:1, :]

    cols_out = pl.ds(pl.multiple_of(i_head * HD, HD), HD)

    def o_copy(zq):
        return remote(
            ou.at[zq], att.at[pl.ds(pl.multiple_of(c * HALF, HALF), HALF), cols_out],
            o_send.at[zq], o_recv.at[i_head, c], at(zq, x, g),
        )

    def o_home(zq):
        return jnp.logical_and(zq == z, c == g)

    def send_o(zq):
        @pl.when(o_home(zq))
        def _():
            pltpu.make_async_copy(
                ou.at[zq], att.at[pl.ds(pl.multiple_of(c * HALF, HALF), HALF), cols_out], o_recv.at[i_head, c]
            ).start()

        @pl.when(jnp.logical_not(o_home(zq)))
        def _():
            o_copy(zq).start()

    def chunk(zq, carry):
        block = 2 * zq + x
        out, row = attend(qu[zq], block * ROWS + c * HALF, block, lambda b: kv[0, b], lambda b: kv[1, b])
        ou[zq] = out
        lg[pl.ds(2 * zq, 1), :] = row[:, :HD]
        lg[pl.ds(2 * zq + 1, 1), :] = row[:, HD:]

        @pl.when(zq > 0)
        def _():
            send_o(jnp.maximum(zq - 1, 0))

        return carry

    lax.fori_loop(0, 3, chunk, 0)
    chain(1)
    lax.fori_loop(3, 6, chunk, 0)
    chain(2)
    lax.fori_loop(6, 8, chunk, 0)
    chain(3)
    send_o(7)

    def lg_copy(t):
        return remote(lg, lg_all.at[i_head, 2 * x + c], lg_send.at[t], lg_recv.at[i_head, 2 * x + c], {"seq": t, "head": 2 * xh + g})

    def lg_here(t):
        return jnp.logical_and(t == seq, c == g)

    def send_lg(t, carry):
        @pl.when(lg_here(t))
        def _():
            pltpu.make_async_copy(lg, lg_all.at[i_head, 2 * x + c], lg_recv.at[i_head, 2 * x + c]).start()

        @pl.when(jnp.logical_not(lg_here(t)))
        def _():
            lg_copy(t).start()

        return carry

    arrived(q5, f_recv.at[2])
    for d in range(-3, 4):

        @pl.when(jnp.logical_and(z + d >= 0, z + d < NZ))
        def _():
            b = 2 * (z + d) + 1 - c
            arrived(kv5.at[b], c5_recv.at[b])

    for h in range(2):
        out, row = attend(
            q5[h * HALF : (h + 1) * HALF, :], kb5 * ROWS + h * HALF, kb5, lambda b: kv5[b, 0], lambda b: kv5[b, 1]
        )
        o5[h * HALF : (h + 1) * HALF, :] = out
        lg5[2 * h : 2 * h + 1, :] = row[:, :HD]
        lg5[2 * h + 1 : 2 * h + 2, :] = row[:, HD:]
        if h == 0:
            lax.fori_loop(0, 16, send_lg, 0)

    def find(b, state):
        count, found = state[0], state[1:]
        mine = plan_ref[b] == seq
        found = tuple(jnp.where(jnp.logical_and(mine, count == n), b, f) for n, f in enumerate(found))
        return (count + jnp.where(mine, 1, 0), *found)

    found = lax.fori_loop(0, 64, find, (0, 0, 0, 0, 0))[1:]

    def lg5_copy(t):
        return remote(lg5, lg5_all.at[kb5], lg5_send.at[t], lg5_recv.at[kb5], {"seq": t, "head": 2 * xh + x})

    def lg5_here(t):
        return jnp.logical_and(t == seq, c == x)

    def send_lg5(t, carry):
        @pl.when(lg5_here(t))
        def _():
            pltpu.make_async_copy(lg5, lg5_all.at[kb5], lg5_recv.at[kb5]).start()

        @pl.when(jnp.logical_not(lg5_here(t)))
        def _():
            lg5_copy(t).start()

        return carry

    lax.fori_loop(0, 16, send_lg5, 0)
    o5_dst = att.at[:, cols5]

    @pl.when(same)
    def _():
        pltpu.make_async_copy(o5, o5_dst, o5_recv).start()

    @pl.when(jnp.logical_not(same))
    def _():
        remote(o5, o5_dst, o5_send, o5_recv, at(z, 1 - x, 1 - c)).start()

    each_piece(sent_piece)
    sent_swap()
    for src in range(NZ):
        to_x(src).wait_send()
    for b in range(16):
        to_core(b).wait_send()
    for d in range(-3, 4):

        @pl.when(jnp.logical_and(z + d >= 0, z + d < NZ))
        def _():
            c5_copy(z + d).wait_send()

    for s in (1, 2, 3):

        @pl.when(goes_right(s))
        def _():
            right(s).wait_send()

        @pl.when(goes_left(s))
        def _():
            left(s).wait_send()

    for zq in range(NZ):

        @pl.when(jnp.logical_not(o_home(zq)))
        def _():
            o_copy(zq).wait_send()

    def sent_lg(t, carry):
        @pl.when(jnp.logical_not(lg_here(t)))
        def _():
            lg_copy(t).wait_send()

        @pl.when(jnp.logical_not(lg5_here(t)))
        def _():
            lg5_copy(t).wait_send()

        return carry

    lax.fori_loop(0, 16, sent_lg, 0)

    @pl.when(jnp.logical_not(same))
    def _():
        remote(o5, o5_dst, o5_send, o5_recv, at(z, 1 - x, 1 - c)).wait_send()

    for i in range(4):
        for w in range(4):
            arrived(lg_all.at[i, w], lg_recv.at[i, w])
    for b in range(16):
        arrived(lg5_all.at[b], lg5_recv.at[b])
    for n, b in enumerate(found):
        w = (b // 2) % 4
        row = 2 * (b // 8) + b % 2
        for i in range(4):
            lg_out[i : i + 1, n * HD : (n + 1) * HD] = lg_all[i, w, pl.ds(row, 1), :]
        lg_out[4:5, n * HD : (n + 1) * HD] = lg5_all[b // 4, pl.ds(b % 4, 1), :]
    for i in range(4):
        for a in range(2):
            arrived(att.at[pl.ds(a * HALF, HALF), pl.ds(i * HD, HD)], o_recv.at[i, a])
    arrived(o5_dst, o5_recv)


def shards(queries, keys, values, clip_ids, plan):
    vmem = pl.BlockSpec(memory_space=pltpu.VMEM)
    anywhere = pl.BlockSpec(memory_space=pl.ANY)
    bf16, f32 = jnp.bfloat16, jnp.float32
    dma = pltpu.SemaphoreType.DMA
    return pl.pallas_call(
        kernel,
        out_shape=(jax.ShapeDtypeStruct((ROWS, 5 * HD), bf16), jax.ShapeDtypeStruct((5, ROWS), f32)),
        in_specs=[anywhere, anywhere, anywhere, vmem, pl.BlockSpec(memory_space=pltpu.SMEM)],
        out_specs=(vmem, vmem),
        scratch_shapes=[
            pltpu.VMEM((2, 2 * NZ, ROWS, HD), bf16),
            pltpu.VMEM((NZ, HALF, HD), bf16),
            pltpu.VMEM((NZ, HALF, HD), bf16),
            pltpu.VMEM((2 * NZ, 2, ROWS, HD), bf16),
            pltpu.VMEM((ROWS, HD), bf16),
            pltpu.VMEM((ROWS, HD), bf16),
            pltpu.VMEM((2 * NZ, ROWS, HD), bf16),
            pltpu.VMEM((HALF, HD), f32),
            pltpu.VMEM((HALF, 2 * HD), f32),
            pltpu.VMEM((2 * NZ, HD), f32),
            pltpu.VMEM((8, HD), f32),
            pltpu.VMEM((4, 4, 2 * NZ, HD), f32),
            pltpu.VMEM((2 * NZ, 8, HD), f32),
            dma((4, 2)), dma((4,)), dma((4,)), dma((NZ,)), dma((2 * NZ,)), dma((3,)), dma((2, 3)), dma((NZ,)),
            dma((NZ,)), dma, dma((16,)), dma((16,)),
            dma((NZ,)), dma((NZ,)), dma((NZ,)), dma((2 * NZ,)), dma((3,)), dma((3,)), dma((3,)), dma((2 * NZ,)),
            dma((4, 2)), dma, dma((4, 4)), dma((16,)),
        ],
        compiler_params=pltpu.CompilerParams(collective_id=0, has_side_effects=True, vmem_limit_bytes=48 << 20),
        name="clips",
    )(queries, keys, values, clip_ids.reshape(64, HD), plan)


def solution(mesh):
    return jax.shard_map(
        shards,
        mesh=mesh,
        in_specs=(
            P(("req", "seq"), "head"),
            P(("req", "seq"), "head"),
            P(("req", "seq"), "head"),
            P("req"),
            P("req"),
        ),
        out_specs=(P(("req", "seq"), "head"), P("head", ("req", "seq"))),
        check_vma=False,
    )
```

time: 1000 us -> 139 us (0.14)
  waiting for transfers between devices: 559 us -> 0 us
  matrix products: 148 us -> 0 us
  blocking collectives: 136 us -> 0 us
  Pallas kernels: 0 us -> 132 us
  local copies, waits for them, and re-layouts: 73.1 us -> 6.11 us
  other arithmetic: 54 us -> 0 us
  between operations: 14.3 us -> 0.65 us
  starting transfers between devices: 12.1 us -> 0 us
    all_gather x2 -> x0, waiting for transfers between devices: 446 us -> none  [the longest x1 228 us: shards(): value_part = lax.all_gather(loop_source[1], 'seq', axis=0, tiled=True)]
    dot_general x32 -> x0, matrix products: 148 us -> none  [the longest x16 92 us: attend_block(): jnp.einsum('hqk,khd->qhd', weights.astype(jnp.bfloat16), value_part.resha...]
    all_to_all x2 -> x0, blocking collectives: 136 us -> none  [the longest x1 70.5 us: shards(): lax.all_to_all(pack_slots(keys, send_pick, send_filled), 'seq', split_axi...]
    pallas_call x0 -> x1, Pallas kernels: none -> 132 us  [shards(): pl.pallas_call(kernel, out_shape=(jax.ShapeDtypeStruct((ROWS, 5 * HD), bf...]
    all_to_all x2 -> x0, waiting for transfers between devices: 112 us -> none  [the longest x1 59.6 us: shards(): lax.all_to_all(pack_slots(finished, back_pick, back_filled), 'seq', split...]
    dynamic_slice x65 -> x0, local copies, waits for them, and re-layouts: 42.8 us -> none  [the longest x64 42.1 us: shards(): final_state, unused = lax.scan(scan_step, start_state, inputs)]
    reduce_sum x22 -> x0, other arithmetic: 21.9 us -> none  [the longest x16 20.3 us: attend_block(): running_sum = running_sum * rescale + jnp.sum(weights, axis=2)]
    gather x10 -> x0, local copies, waits for them, and re-layouts: 18.3 us -> none  [the longest x4 9.4 us: read_slots(): jnp.take(arrived.reshape(slot_count, BLOCK, columns), picked, axis=0)]
  transfers between devices with their start and end apart: 4 -> 0, of which waited for: 4 -> 0; matrix products, arithmetic and copies ran while one was open for 1% -> 0% of each run, Pallas kernels for 0% -> 0%
where the time goes in v1:
time: 139 us; the launch traced here: 138 us
  Pallas kernels  132 us (95%)
  local copies, waits for them, and re-layouts  6.11 us (4%)
    pallas_call x1, Pallas kernels, shards(): pl.pallas_call(kernel, out_shape=(jax.ShapeDtypeStruct((ROWS, 5 * HD), bf...  132 us
    unnamed x12, local copies, waits for them, and re-layouts  6.11 us

profile of v1, /device:TPU:1, one launch (start us, length us, event | category | flops | bytes accessed | tf_op | source)
XLA Modules:
  0.0 138.3 jit_solution(18287385716697519681)
XLA Ops:
  0.6 0.0 copy-start.4
  0.6 0.6 copy-done.4
  1.3 0.0 copy-start
  1.3 1.1 copy-done
  2.4 0.0 copy-start.1
  2.4 1.1 copy-done.1
  3.5 0.0 copy-start.2
  3.5 1.1 copy-done.2
  4.6 0.0 copy-start.3
  4.6 0.8 copy-done.3
  5.3 131.6 %clips.1 = (bf16[512,640]{1,0:T(8,128)(2,1)S(1)}, f32[5,512]{1,0:T(8,128)S(1)}) custom-call(bf16[512,640]{1,0:T(8,128)(2,1)S(1)} %copy-done, bf16[512,640]{1,0:T(8,128)(2,1)S(1)} %copy-done.1, bf16[512,640]{1,0:T(8,128)(2,1)S(1)} %copy-done.2, s32[64,128]{1,0:T(8,128)S(1)} %bitcast.1, s32[64]{0:T(128)S(1)} %copy-done.4), custom_call_target="tpu_custom_call" | custom-call | tf_op jit(solution)/shard_map/clips/pallas_call | solution.py:439
  136.9 0.8 copy.9
  137.7 0.6 copy.10
Async XLA Ops:
  0.6 0.7 copy-start.4
  1.3 1.1 copy-start
  2.4 1.1 copy-start.1
  3.5 1.1 copy-start.2
  4.6 0.8 copy-start.3

commit v2 on v1

--- a/solution.py
+++ b/solution.py
@@ -11,7 +11,6 @@
 ROWS = 512
 HALF = 256
 NZ = 8
-REACH = 6
 APART = 32768.0
 SCALE = 1.0 / HD**0.5
 TO_EXP2 = 1.4426950408889634 * SCALE
@@ -21,7 +20,7 @@
 def kernel(
     q_in, k_in, v_in, ids_ref, plan_ref,
     att, lg_out,
-    kv, qu, ou, kv5, q5, o5, mk, m_ref, acc_ref, lg, lg5, lg_all, lg5_all,
+    kv, qu, ou, kv5, q5, o5, mk, mq, m_all, acc_all, lg, lg5, lg_all, lg5_all,
     q_send, k_send, v_send, x_send, c_send, f_send, ch_send, c5_send, o_send, o5_send, lg_send, lg5_send,
     q_recv, kv_recv, x_recv, c_recv, f_recv, chl_recv, chr_recv, c5_recv, o_recv, o5_recv, lg_recv, lg5_recv,
 ):
@@ -59,20 +58,22 @@
     lax.fori_loop(0, 32, greet, 0)
     pl.semaphore_wait(barrier, 31)
 
-    def piece(kind, j):
-        cols = pl.ds(j * HD, HD)
-        zt = 2 * j + c
+    odd = (z + c) % 2
+
+    def piece(kind, n):
+        d = (odd, 2 - 3 * odd, 5 * odd - 2, 4 - 7 * odd)[n]
+        zt = (z + d + NZ) % NZ
+        cols = pl.ds(pl.multiple_of((zt // 2) * HD, HD), HD)
         if kind == "k":
-            return k_in.at[:, cols], kv.at[0, 2 * z + x], k_send.at[j], kv_recv.at[z], zt, 0
+            return k_in.at[:, cols], kv.at[0, 2 * z + x], k_send.at[n], kv_recv.at[z], zt, 0
         if kind == "v":
-            return v_in.at[:, cols], kv.at[1, 2 * z + x], v_send.at[j], kv_recv.at[z], zt, 1
-        a = int(kind[1])
-        return q_in.at[pl.ds(a * HALF, HALF), cols], qu.at[z], q_send.at[j, a], q_recv.at[z], zt, a
+            return v_in.at[:, cols], kv.at[1, 2 * z + x], v_send.at[n], kv_recv.at[z], zt, 1
+        return q_in.at[:, cols], qu.at[z // 2], q_send.at[n], q_recv.at[z // 2], zt, z % 2
 
     def each_piece(do):
-        for kind in ("k", "v", "q0", "q1"):
-            for j in range(4):
-                do(*piece(kind, j))
+        for n in range(4):
+            for kind in ("k", "v", "q"):
+                do(*piece(kind, n))
 
     def start_piece(src, dst, send, recv, zt, core):
         here = jnp.logical_and(zt == z, c == core)
@@ -126,16 +127,23 @@
     ids = ids_ref[...]
     starts = [jnp.sum(jnp.sum(jnp.where(ids < n, 1.0, 0.0), axis=0, keepdims=True), axis=1, keepdims=True) for n in (1, 2, 3)]
 
-    def clip_of(first, rows):
-        pos = (first + lax.broadcasted_iota(jnp.int32, (rows, HD), 0)).astype(jnp.float32)
-        clip = jnp.zeros((rows, HD), jnp.float32)
+    def clip_of(block):
+        pos = (block * ROWS + lax.broadcasted_iota(jnp.int32, (ROWS, HD), 0)).astype(jnp.float32)
+        clip = jnp.zeros((ROWS, HD), jnp.float32)
         for s in starts:
             clip = clip + jnp.where(pos >= s, 1.0, 0.0)
-        return clip, lax.broadcasted_iota(jnp.int32, (rows, HD), 1).astype(jnp.float32)
+        return clip, lax.broadcasted_iota(jnp.int32, (ROWS, HD), 1).astype(jnp.float32)
 
     def fill(b, carry):
-        clip, lane = clip_of(b * ROWS, ROWS)
+        clip, lane = clip_of(b)
         mk[b] = jnp.where(lane == clip, 0.0, jnp.where(lane < 4.0, 1.0, 0.0)).astype(jnp.bfloat16)
+        return carry
+
+    def fill_q(n, carry):
+        clip, lane = clip_of(jnp.where(n == 4, kb5, 2 * (2 * n + c) + x))
+        mq[n] = jnp.where(lane == clip, -APART, 0.0).astype(jnp.bfloat16)
+        m_all[n] = jnp.full((ROWS, HD), -1e30, jnp.float32)
+        acc_all[n] = jnp.zeros((ROWS, 2 * HD), jnp.float32)
         return carry
 
     def block_in(src):
@@ -147,14 +155,12 @@
     def to_core(b):
         return remote(kv.at[c, b], kv.at[c, b], c_send.at[b], c_recv.at[b], at(z, x, 1 - c))
 
-    def relay(d):
-        src = (z + d + NZ) % NZ
+    def relay(src):
         arrived(block_in(src), kv_recv.at[src])
         to_x(src).start()
         to_core(2 * src + x).start()
 
-    def relay_x(d):
-        src = (z + d + NZ) % NZ
+    def relay_x(src):
         b = 2 * src + 1 - x
         arrived(kv.at[c, b], x_recv.at[src])
         to_core(b).start()
@@ -177,36 +183,10 @@
     def goes_left(s):
         return jnp.logical_and(z - 1 >= 0, z + s - 1 < NZ)
 
-    lax.fori_loop(0, 16, fill, 0)
-    order = (0, 1, -1, 2, -2, 3, -3, 4)
-    for d in order[:3]:
-        relay(d)
-    arrived(kv5.at[kb5, 0], f_recv.at[0])
-    arrived(kv5.at[kb5, 1], f_recv.at[1])
-    c5_copy(z).start()
-
-    @pl.when(goes_right(1))
-    def _():
-        right(1).start()
-
-    @pl.when(goes_left(1))
-    def _():
-        left(1).start()
-
-    for d in order[3:]:
-        relay(d)
-    for d in order:
-        relay_x(d)
-    for src in range(NZ):
-        arrived(qu.at[src], q_recv.at[src])
-    for b in range(16):
-        arrived(kv.at[1 - c, b], c_recv.at[b])
-
     def chain(s):
         @pl.when(z - s >= 0)
         def _():
-            b = 2 * (z - s) + c
-            arrived(kv5.at[b], chl_recv.at[s - 1])
+            arrived(kv5.at[2 * (z - s) + c], chl_recv.at[s - 1])
             c5_copy(z - s).start()
 
         if s < 3:
@@ -217,8 +197,7 @@
 
         @pl.when(z + s < NZ)
         def _():
-            b = 2 * (z + s) + c
-            arrived(kv5.at[b], chr_recv.at[s - 1])
+            arrived(kv5.at[2 * (z + s) + c], chr_recv.at[s - 1])
             c5_copy(z + s).start()
 
         if s < 3:
@@ -227,76 +206,129 @@
             def _():
                 left(s + 1).start()
 
-    ones = jnp.ones((ROWS, HD), jnp.bfloat16)
-
-    def attend(q, first, block, k_of, v_of):
-        clip, lane = clip_of(first, HALF)
-        mq = jnp.where(lane == clip, -APART, 0.0).astype(jnp.bfloat16)
-        qa = jnp.concatenate([q, mq], axis=1)
-        m_ref[...] = jnp.full((HALF, HD), -1e30, jnp.float32)
-        acc_ref[...] = jnp.zeros((HALF, 2 * HD), jnp.float32)
-
-        def step(b, carry):
-            ka = jnp.concatenate([k_of(b), mk[b]], axis=1)
-            s = lax.dot_general(qa, ka, (((1,), (1,)), ((), ())), preferred_element_type=jnp.float32)
-            m_old = m_ref[...]
-            m_new = jnp.maximum(m_old, jnp.max(s, axis=1, keepdims=True))
+    def offset(t):
+        return ((t + 1) // 2) * (2 * (t % 2) - 1)
+
+    def source(t):
+        return (z + offset(t) + NZ) % NZ
+
+    ones = jnp.ones((2 * ROWS, HD), jnp.bfloat16)
+
+    def tile(n, q, zk, k_of, v_of):
+        keys = [jnp.concatenate([k_of(2 * zk + l), mk[2 * zk + l]], axis=1) for l in range(2)]
+        va = jnp.concatenate([jnp.concatenate([v_of(2 * zk), v_of(2 * zk + 1)], axis=0), ones], axis=1)
+        for h in range(2):
+            part = slice(h * HALF, (h + 1) * HALF)
+            qa = jnp.concatenate([q[part, :], mq[n, part, :]], axis=1)
+            scores = [
+                lax.dot_general(qa, k, (((1,), (1,)), ((), ())), preferred_element_type=jnp.float32) for k in keys
+            ]
+            top = functools.reduce(
+                jnp.maximum, [s[:, l * HD : (l + 1) * HD] for s in scores for l in range(ROWS // HD)]
+            )
+            m_old = m_all[n, part, :]
+            m_new = jnp.maximum(m_old, jnp.max(top, axis=1, keepdims=True))
             alpha = jnp.exp2((m_old - m_new) * TO_EXP2)
-            p = jnp.exp2((s - jnp.concatenate([m_new] * (ROWS // HD), axis=1)) * TO_EXP2)
-            va = jnp.concatenate([v_of(b), ones], axis=1)
-            pv = jnp.dot(p.astype(jnp.bfloat16), va, preferred_element_type=jnp.float32)
-            acc_ref[...] = acc_ref[...] * jnp.concatenate([alpha, alpha], axis=1) + pv
-            m_ref[...] = m_new
-            return carry
-
-        lax.fori_loop(jnp.maximum(block - REACH, 0), jnp.minimum(block + REACH + 1, 2 * NZ), step, 0)
-        total = acc_ref[:, HD:]
-        out = (acc_ref[:, :HD] / total).astype(jnp.bfloat16)
-        log_total = m_ref[...] * SCALE + jnp.log(total)
-        return out, jnp.transpose(log_total)[0:1, :]
+            m_wide = jnp.concatenate([m_new] * (ROWS // HD), axis=1)
+            p = jnp.concatenate([jnp.exp2((s - m_wide) * TO_EXP2).astype(jnp.bfloat16) for s in scores], axis=1)
+            pv = jnp.dot(p, va, preferred_element_type=jnp.float32)
+            acc_all[n, part, :] = acc_all[n, part, :] * jnp.concatenate([alpha, alpha], axis=1) + pv
+            m_all[n, part, :] = m_new
+
+    def finish(n):
+        total = acc_all[n, :, HD:]
+        out = (acc_all[n, :, :HD] / total).astype(jnp.bfloat16)
+        rows = jnp.transpose(m_all[n] * SCALE + jnp.log(total))[0:1, :]
+        return out, [rows[:, r * HD : (r + 1) * HD] for r in range(ROWS // HD)]
 
     cols_out = pl.ds(pl.multiple_of(i_head * HD, HD), HD)
 
-    def o_copy(zq):
-        return remote(
-            ou.at[zq], att.at[pl.ds(pl.multiple_of(c * HALF, HALF), HALF), cols_out],
-            o_send.at[zq], o_recv.at[i_head, c], at(zq, x, g),
-        )
-
-    def o_home(zq):
-        return jnp.logical_and(zq == z, c == g)
-
-    def send_o(zq):
-        @pl.when(o_home(zq))
-        def _():
-            pltpu.make_async_copy(
-                ou.at[zq], att.at[pl.ds(pl.multiple_of(c * HALF, HALF), HALF), cols_out], o_recv.at[i_head, c]
-            ).start()
-
-        @pl.when(jnp.logical_not(o_home(zq)))
-        def _():
-            o_copy(zq).start()
-
-    def chunk(zq, carry):
-        block = 2 * zq + x
-        out, row = attend(qu[zq], block * ROWS + c * HALF, block, lambda b: kv[0, b], lambda b: kv[1, b])
-        ou[zq] = out
-        lg[pl.ds(2 * zq, 1), :] = row[:, :HD]
-        lg[pl.ds(2 * zq + 1, 1), :] = row[:, HD:]
-
-        @pl.when(zq > 0)
-        def _():
-            send_o(jnp.maximum(zq - 1, 0))
-
-        return carry
-
-    lax.fori_loop(0, 3, chunk, 0)
+    def o_dst():
+        return att.at[:, cols_out]
+
+    def o_copy(n):
+        return remote(ou.at[n], o_dst(), o_send.at[n], o_recv.at[i_head], at(2 * n + c, x, g))
+
+    def o_home(n):
+        return jnp.logical_and(2 * n + c == z, c == g)
+
+    def send_o(n):
+        @pl.when(o_home(n))
+        def _():
+            pltpu.make_async_copy(ou.at[n], o_dst(), o_recv.at[i_head]).start()
+
+        @pl.when(jnp.logical_not(o_home(n)))
+        def _():
+            o_copy(n).start()
+
+    lax.fori_loop(0, 16, fill, 0)
+    lax.fori_loop(0, 5, fill_q, 0)
+    relay(source(0))
+    relay_x(source(0))
+
+    def stage(j, carry):
+        s_j = source(j)
+
+        @pl.when(j < 7)
+        def _():
+            relay(source(jnp.minimum(j + 1, 7)))
+
+        @pl.when(j == 1)
+        def _():
+            arrived(kv5.at[kb5, 0], f_recv.at[0])
+            arrived(kv5.at[kb5, 1], f_recv.at[1])
+            arrived(q5, f_recv.at[2])
+            c5_copy(z).start()
+
+            @pl.when(goes_right(1))
+            def _():
+                right(1).start()
+
+            @pl.when(goes_left(1))
+            def _():
+                left(1).start()
+
+        for l in range(2):
+            arrived(kv.at[1 - c, 2 * s_j + l], c_recv.at[2 * s_j + l])
+
+        @pl.when(s_j % 2 == c)
+        def _():
+            arrived(qu.at[s_j // 2], q_recv.at[s_j // 2])
+
+        @pl.when(j < 7)
+        def _():
+            relay_x(source(jnp.minimum(j + 1, 7)))
+
+        return carry
+
+    lax.fori_loop(0, 8, stage, 0)
+
+    def chunk(n, carry):
+        zq = 2 * n + c
+
+        def step(zk, inner):
+            tile(n, qu.at[n], zk, lambda b: kv[0, b], lambda b: kv[1, b])
+            return inner
+
+        lax.fori_loop(jnp.maximum(zq - 3, 0), jnp.minimum(zq + 4, NZ), step, 0)
+        out, rows = finish(n)
+        ou[n] = out
+        for r in range(4):
+            lg[pl.ds(4 * n + r, 1), :] = rows[r]
+
+        @pl.when(n > 0)
+        def _():
+            send_o(jnp.maximum(n - 1, 0))
+
+        return carry
+
     chain(1)
-    lax.fori_loop(3, 6, chunk, 0)
+    lax.fori_loop(0, 1, chunk, 0)
     chain(2)
-    lax.fori_loop(6, 8, chunk, 0)
+    lax.fori_loop(1, 2, chunk, 0)
     chain(3)
-    send_o(7)
+    lax.fori_loop(2, 4, chunk, 0)
+    send_o(3)
 
     def lg_copy(t):
         return remote(lg, lg_all.at[i_head, 2 * x + c], lg_send.at[t], lg_recv.at[i_head, 2 * x + c], {"seq": t, "head": 2 * xh + g})
@@ -315,23 +347,27 @@
 
         return carry
 
-    arrived(q5, f_recv.at[2])
-    for d in range(-3, 4):
-
-        @pl.when(jnp.logical_and(z + d >= 0, z + d < NZ))
-        def _():
-            b = 2 * (z + d) + 1 - c
+    lax.fori_loop(0, 16, send_lg, 0)
+    def own_there(t, carry):
+        zk = z + offset(t)
+
+        @pl.when(jnp.logical_and(zk >= 0, zk < NZ))
+        def _():
+            b = 2 * zk + 1 - c
             arrived(kv5.at[b], c5_recv.at[b])
 
-    for h in range(2):
-        out, row = attend(
-            q5[h * HALF : (h + 1) * HALF, :], kb5 * ROWS + h * HALF, kb5, lambda b: kv5[b, 0], lambda b: kv5[b, 1]
-        )
-        o5[h * HALF : (h + 1) * HALF, :] = out
-        lg5[2 * h : 2 * h + 1, :] = row[:, :HD]
-        lg5[2 * h + 1 : 2 * h + 2, :] = row[:, HD:]
-        if h == 0:
-            lax.fori_loop(0, 16, send_lg, 0)
+        return carry
+
+    def own(zk, carry):
+        tile(4, q5, zk, lambda b: kv5[b, 0], lambda b: kv5[b, 1])
+        return carry
+
+    lax.fori_loop(0, 7, own_there, 0)
+    lax.fori_loop(jnp.maximum(z - 3, 0), jnp.minimum(z + 4, NZ), own, 0)
+    out, rows = finish(4)
+    o5[...] = out
+    for r in range(4):
+        lg5[r : r + 1, :] = rows[r]
 
     def find(b, state):
         count, found = state[0], state[1:]
@@ -391,11 +427,11 @@
         def _():
             left(s).wait_send()
 
-    for zq in range(NZ):
-
-        @pl.when(jnp.logical_not(o_home(zq)))
-        def _():
-            o_copy(zq).wait_send()
+    for n in range(4):
+
+        @pl.when(jnp.logical_not(o_home(n)))
+        def _(n=n):
+            o_copy(n).wait_send()
 
     def sent_lg(t, carry):
         @pl.when(jnp.logical_not(lg_here(t)))
@@ -420,14 +456,13 @@
     for b in range(16):
         arrived(lg5_all.at[b], lg5_recv.at[b])
     for n, b in enumerate(found):
-        w = (b // 2) % 4
-        row = 2 * (b // 8) + b % 2
+        w = 2 * ((b // 4) % 2) + (b // 8) % 2
+        row = 4 * (b // 16) + b % 4
         for i in range(4):
             lg_out[i : i + 1, n * HD : (n + 1) * HD] = lg_all[i, w, pl.ds(row, 1), :]
         lg_out[4:5, n * HD : (n + 1) * HD] = lg5_all[b // 4, pl.ds(b % 4, 1), :]
     for i in range(4):
-        for a in range(2):
-            arrived(att.at[pl.ds(a * HALF, HALF), pl.ds(i * HD, HD)], o_recv.at[i, a])
+        arrived(att.at[:, pl.ds(i * HD, HD)], o_recv.at[i])
     arrived(o5_dst, o5_recv)
 
 
@@ -443,24 +478,25 @@
         out_specs=(vmem, vmem),
         scratch_shapes=[
             pltpu.VMEM((2, 2 * NZ, ROWS, HD), bf16),
-            pltpu.VMEM((NZ, HALF, HD), bf16),
-            pltpu.VMEM((NZ, HALF, HD), bf16),
+            pltpu.VMEM((4, ROWS, HD), bf16),
+            pltpu.VMEM((4, ROWS, HD), bf16),
             pltpu.VMEM((2 * NZ, 2, ROWS, HD), bf16),
             pltpu.VMEM((ROWS, HD), bf16),
             pltpu.VMEM((ROWS, HD), bf16),
             pltpu.VMEM((2 * NZ, ROWS, HD), bf16),
-            pltpu.VMEM((HALF, HD), f32),
-            pltpu.VMEM((HALF, 2 * HD), f32),
+            pltpu.VMEM((5, ROWS, HD), bf16),
+            pltpu.VMEM((5, ROWS, HD), f32),
+            pltpu.VMEM((5, ROWS, 2 * HD), f32),
             pltpu.VMEM((2 * NZ, HD), f32),
             pltpu.VMEM((8, HD), f32),
             pltpu.VMEM((4, 4, 2 * NZ, HD), f32),
             pltpu.VMEM((2 * NZ, 8, HD), f32),
-            dma((4, 2)), dma((4,)), dma((4,)), dma((NZ,)), dma((2 * NZ,)), dma((3,)), dma((2, 3)), dma((NZ,)),
-            dma((NZ,)), dma, dma((16,)), dma((16,)),
-            dma((NZ,)), dma((NZ,)), dma((NZ,)), dma((2 * NZ,)), dma((3,)), dma((3,)), dma((3,)), dma((2 * NZ,)),
-            dma((4, 2)), dma, dma((4, 4)), dma((16,)),
+            dma((4,)), dma((4,)), dma((4,)), dma((NZ,)), dma((2 * NZ,)), dma((3,)), dma((2, 3)), dma((NZ,)),
+            dma((4,)), dma, dma((16,)), dma((16,)),
+            dma((4,)), dma((NZ,)), dma((NZ,)), dma((2 * NZ,)), dma((3,)), dma((3,)), dma((3,)), dma((2 * NZ,)),
+            dma((4,)), dma, dma((4, 4)), dma((16,)),
         ],
-        compiler_params=pltpu.CompilerParams(collective_id=0, has_side_effects=True, vmem_limit_bytes=48 << 20),
+        compiler_params=pltpu.CompilerParams(collective_id=0, has_side_effects=True, vmem_limit_bytes=67043328),
         name="clips",
     )(queries, keys, values, clip_ids.reshape(64, HD), plan)
 

time: 139 us -> 107 us (0.77)
  Pallas kernels: 132 us -> 103 us
  local copies, waits for them, and re-layouts: 6.11 us -> 2.59 us
    pallas_call x1, Pallas kernels: 132 us -> 103 us  [shards(): pl.pallas_call(kernel, out_shape=(jax.ShapeDtypeStruct((ROWS, 5 * HD), bf...]
    unnamed x12 -> x4, local copies, waits for them, and re-layouts: 6.11 us -> 2.59 us
where the time goes in v2:
time: 107 us; the launch traced here: 106 us
  Pallas kernels  103 us (96%)
  local copies, waits for them, and re-layouts  2.59 us (2%)
    pallas_call x1, Pallas kernels, shards(): pl.pallas_call(kernel, out_shape=(jax.ShapeDtypeStruct((ROWS, 5 * HD), bf...  103 us
    unnamed x4, local copies, waits for them, and re-layouts  2.59 us

profile of v2, /device:TPU:1, one launch (start us, length us, event | category | flops | bytes accessed | tf_op | source)
XLA Modules:
  0.0 106.4 jit_solution(2711337592942050271)
XLA Ops:
  0.6 103.1 %clips.1 = (bf16[512,640]{1,0:T(8,128)(2,1)}, f32[5,512]{1,0:T(8,128)}) custom-call(bf16[512,640]{1,0:T(8,128)(2,1)} %q_in.1, bf16[512,640]{1,0:T(8,128)(2,1)} %k_in.1, bf16[512,640]{1,0:T(8,128)(2,1)} %v_in.1, s32[64,128]{1,0:T(8,128)} %bitcast.1, s32[64]{0:T(128)} %plan_ref.1), custom_call_target="tpu_custom_call" | custom-call | tf_op jit(solution)/shard_map/clips/pallas_call | solution.py:474
  103.8 0.0 copy-start
  103.8 2.0 %copy.9 = bf16[512,640]{1,0:T(8,128)(2,1)} copy(bf16[512,640]{1,0:T(8,128)(2,1)} %get-tuple-element.4) | data formatting | bytes 1310720
  105.8 0.0 copy-done
  105.8 0.6 copy.10
Async XLA Ops:
  103.8 2.0 %copy-start = (f32[5,512]{1,0:T(8,128)S(1)}, f32[5,512]{1,0:T(8,128)}, u32[]{:S(2)}) copy-start(f32[5,512]{1,0:T(8,128)} %get-tuple-element.5) | copy-start | bytes 30724

commit v3 on v2

--- a/solution.py
+++ b/solution.py
@@ -263,6 +263,14 @@
 
     lax.fori_loop(0, 16, fill, 0)
     lax.fori_loop(0, 5, fill_q, 0)
+    def find(b, state):
+        count, found = state[0], state[1:]
+        mine = plan_ref[b] == seq
+        found = tuple(jnp.where(jnp.logical_and(mine, count == n), b, f) for n, f in enumerate(found))
+        return (count + jnp.where(mine, 1, 0), *found)
+
+    found = lax.fori_loop(0, 64, find, (0, 0, 0, 0, 0))[1:]
+
     relay(source(0))
     relay_x(source(0))
 
@@ -369,14 +377,6 @@
     for r in range(4):
         lg5[r : r + 1, :] = rows[r]
 
-    def find(b, state):
-        count, found = state[0], state[1:]
-        mine = plan_ref[b] == seq
-        found = tuple(jnp.where(jnp.logical_and(mine, count == n), b, f) for n, f in enumerate(found))
-        return (count + jnp.where(mine, 1, 0), *found)
-
-    found = lax.fori_loop(0, 64, find, (0, 0, 0, 0, 0))[1:]
-
     def lg5_copy(t):
         return remote(lg5, lg5_all.at[kb5], lg5_send.at[t], lg5_recv.at[kb5], {"seq": t, "head": 2 * xh + x})
 
@@ -394,7 +394,6 @@
 
         return carry
 
-    lax.fori_loop(0, 16, send_lg5, 0)
     o5_dst = att.at[:, cols5]
 
     @pl.when(same)
@@ -404,6 +403,8 @@
     @pl.when(jnp.logical_not(same))
     def _():
         remote(o5, o5_dst, o5_send, o5_recv, at(z, 1 - x, 1 - c)).start()
+
+    lax.fori_loop(0, 16, send_lg5, 0)
 
     each_piece(sent_piece)
     sent_swap()

time: 107 us -> 106 us (level)
  no operation moved by 1% of the time
where the time goes in v3:
time: 106 us
  Pallas kernels  102 us (96%)
  local copies, waits for them, and re-layouts  2.59 us (2%)
    pallas_call x1, Pallas kernels, shards(): pl.pallas_call(kernel, out_shape=(jax.ShapeDtypeStruct((ROWS, 5 * HD), bf...  102 us
    unnamed x4, local copies, waits for them, and re-layouts  2.59 us

profile of v3, /device:TPU:1, one launch (start us, length us, event | category | flops | bytes accessed | tf_op | source)
XLA Modules:
  0.0 105.6 jit_solution(16502441255473296333)
XLA Ops:
  0.6 102.3 %clips.1 = (bf16[512,640]{1,0:T(8,128)(2,1)}, f32[5,512]{1,0:T(8,128)}) custom-call(bf16[512,640]{1,0:T(8,128)(2,1)} %q_in.1, bf16[512,640]{1,0:T(8,128)(2,1)} %k_in.1, bf16[512,640]{1,0:T(8,128)(2,1)} %v_in.1, s32[64,128]{1,0:T(8,128)} %bitcast.1, s32[64]{0:T(128)} %plan_ref.1), custom_call_target="tpu_custom_call" | custom-call | tf_op jit(solution)/shard_map/clips/pallas_call | solution.py:475
  103.0 0.0 copy-start
  103.0 2.0 %copy.9 = bf16[512,640]{1,0:T(8,128)(2,1)} copy(bf16[512,640]{1,0:T(8,128)(2,1)} %get-tuple-element.4) | data formatting | bytes 1310720
  105.0 0.0 copy-done
  105.0 0.6 copy.10
Async XLA Ops:
  103.0 2.0 %copy-start = (f32[5,512]{1,0:T(8,128)S(1)}, f32[5,512]{1,0:T(8,128)}, u32[]{:S(2)}) copy-start(f32[5,512]{1,0:T(8,128)} %get-tuple-element.5) | copy-start | bytes 30724
